TPU v7x, 128 devices: a whole 4x4x4 slice. The times are simulated.
128 devices in a mesh: gx: 8 (over y, core), gy: 16 (over z, x).
Axes of the slice: x: 4, y: 4, z: 4, core: 2. Of those that a mesh axis runs over, the one named last changes fastest.
Arguments:
- thermal_anomaly: float32 [32, 256, 2048], P(None, 'gx', 'gy'), may hold values from -6 to 6
- ambient_diffusion: bfloat16 [256, 2048], P('gx', 'gy'), may hold values from 0.019897461 to 0.25
- solar_light: bfloat16 [256, 2048], P('gx', 'gy'), may hold values from 0.5 to 4
- sea_tile_flags: int32 [8, 16, 64], P('gx', 'gy'), may hold values 0 or 1
- flooded_layer_tally: int32 [8, 16, 64], P('gx', 'gy'), may hold values from 1 to 32
- tile_holder_rank: int32 [8, 16, 64, 1], P('gx', 'gy'), may hold values from 0 to 15; in each aligned block of 64 rows (0 to 63, 64 to 127, ..., all dimensions but the last counted through in order) at most 8 rows name the same one
- solute_amounts: float32 [8, 16, 128, 8, 2048], P('gx', 'gy'), may hold values from 0.09 to 11
- reaction_rates: float32 [8, 8], replicated, may hold values from -0.2 to 0.5
Outputs:
- thermal_final: float32 [32, 256, 2048], P(None, 'gx', 'gy')
- solute_final: float32 [8, 16, 128, 8, 2048], P('gx', 'gy')
Inputs may be any that keep to these rules, and one draw needn't show every extreme that they name: `tile_holder_rank`: among the 64 blocks of one device, at most 8 name the same owner, a bound that some block reaches of them.
All inputs are finite; a program needn't handle non-finite values. No bound on the sum of `sea_tile_flags` on one device may be relied on, other than what follows from the above.
Results may differ from a plain program's by a relative error of at most 0.0003.
Values may be sent and summed in bfloat16 or wider, within the bound.
A program may use at most 128 MiB of HBM per device.

v0:
```python
import jax
import jax.numpy as jnp
from jax import lax
from jax.sharding import Mesh
from jax.sharding import PartitionSpec as P

GX_GY = ("gx_0", "gx_1", "gy_0", "gy_1")
GX = ("gx_0", "gx_1")
GY = ("gy_0", "gy_1")
NU_COEF = 0.2
STEP_DT = 0.05
ATTEN_WATER = 0.06
ATTEN_CHL = 0.05
WARMING_SCALE = 0.5
GROWTH_TEMP = 0.063


def with_halo(shard, sides, width):
    edges = {}
    for axis, dim in sides:
        count, length = (lax.axis_size(axis), shard.shape[dim])
        up = [(i, (i + 1) % count) for i in range(count - 1)]
        last = lax.slice_in_dim(shard, length - width, length, axis=dim)
        initial = lax.slice_in_dim(shard, 0, width, axis=dim)
        edges[dim] = (
            lax.ppermute(last, axis, up),
            lax.ppermute(initial, axis, [(b, a) for a, b in up]),
        )
    done = []
    for _, dim in sides:
        low, high = edges[dim]
        around = [(width, width) if d in done else (0, 0) for d in range(shard.ndim)]
        shard = jnp.concatenate([jnp.pad(low, around), shard, jnp.pad(high, around)], axis=dim)
        done.append(dim)
    return shard


def by_axis(shard, axes):
    for axis in axes:
        shard = lax.psum(shard, axis)
    return shard


def masked_step(field, within_layer):
    center = field[:, 1:-1, 1:-1]
    span_east = center.shape[1]
    span_north = center.shape[2]
    total = jnp.zeros_like(center)
    for first, second in ((0, 1), (2, 1), (1, 0), (1, 2)):
        near = field[:, first : first + span_east, second : second + span_north]
        total = total + within_layer[:, first : first + span_east, second : second + span_north] * (
            near - center
        )
    return center + NU_COEF * within_layer[:, 1:-1, 1:-1] * total


def level_below(values):
    return jnp.concatenate([values[..., 64:], values[..., -64:]], axis=-1)


def level_above_zero(values):
    return jnp.concatenate([jnp.zeros_like(values[..., :64]), values[..., :-64]], axis=-1)


def level_prefix(values, layer_tally):
    running = values
    reach = 1
    while reach < layer_tally:
        moved = jnp.concatenate(
            [jnp.zeros_like(running[..., : 64 * reach]), running[..., : -64 * reach]], axis=-1
        )
        running = running + moved
        reach = reach * 2
    return running


def spread_levels(column_values, layer_tally):
    return jnp.tile(column_values, (1, layer_tally))


def flat_mixer(temp_flat, kbg_flat):
    return (kbg_flat * (1.0 + 0.5 * jnp.tanh(temp_flat - level_below(temp_flat)))).astype(
        jnp.bfloat16
    )


def flat_validity(tile_amount, flat_width):
    levels = lax.broadcasted_iota(jnp.int32, (1, flat_width), 1) // 64
    valid = (levels < tile_amount[:, None]).astype(jnp.float32)
    active = (levels + 1 < tile_amount[:, None]).astype(jnp.float32)
    return (valid, active)


def totals(amounts_on_chip, valid):
    return jnp.sum(amounts_on_chip * valid[:, None], axis=(0, 2))


def column_step(
    temp_flat, kappa_flat, surface, valid, active, amounts_on_chip, reaction_rates, layer_tally
):
    atten = ATTEN_WATER + ATTEN_CHL * amounts_on_chip[:, 0]
    cumul = level_prefix(atten, layer_tally)
    top = surface * jnp.exp(-(cumul - atten))
    bottom = surface * jnp.exp(-cumul)
    heat = (valid * (top - bottom)).astype(jnp.bfloat16)
    growth = jnp.exp(GROWTH_TEMP * temp_flat.astype(jnp.float32)) * top / (top + 1.0)
    mixed = jnp.einsum(
        "rs,nsf->nrf", reaction_rates, amounts_on_chip, precision=lax.Precision.HIGHEST
    )
    flux = (kappa_flat.astype(jnp.float32) * active)[:, None] * (
        level_below(amounts_on_chip) - amounts_on_chip
    )
    new = amounts_on_chip + valid[:, None] * STEP_DT * (
        flux - level_above_zero(flux) + growth[:, None] * mixed
    )
    return (new, heat)


def plane_blocks(field, blocks_x, blocks_y):
    return (
        field.reshape(blocks_x, 8, blocks_y, 8)
        .transpose(0, 2, 1, 3)
        .reshape(blocks_x * blocks_y, 64)
    )


def on_device(
    thermal_anomaly,
    ambient_diffusion,
    solar_light,
    sea_tile_flags,
    flooded_layer_tally,
    tile_holder_rank,
    solute_amounts,
    reaction_rates,
):
    layer_tally = thermal_anomaly.shape[0]
    span_east = thermal_anomaly.shape[1]
    span_north = thermal_anomaly.shape[2]
    blocks_x = span_east // 8
    blocks_y = span_north // 8
    tile_summation = blocks_x * blocks_y
    flat_width = layer_tally * 64
    depth_block = (sea_tile_flags * flooded_layer_tally).reshape(tile_summation)
    cell_count = jnp.repeat(
        jnp.repeat(depth_block.reshape(blocks_x, blocks_y), 8, axis=0), 8, axis=1
    )
    level_idx = lax.broadcasted_iota(jnp.int32, (layer_tally, 1, 1), 0)
    joined = jnp.concatenate([thermal_anomaly, cell_count[None].astype(jnp.float32)], axis=0)
    padded = with_halo(joined, ((GX, 1), (GY, 2)), 1)
    inside_pad = (level_idx.astype(jnp.float32) < padded[layer_tally : layer_tally + 1]).astype(
        jnp.float32
    )
    advanced_verticals = masked_step(padded[:layer_tally], inside_pad)
    dispatched = advanced_verticals.astype(jnp.bfloat16)
    thermal_tiles = (
        dispatched.reshape(layer_tally, blocks_x, 8, blocks_y, 8)
        .transpose(1, 3, 0, 2, 4)
        .reshape(tile_summation, flat_width)
    )
    ambient_diffusion_tiles = plane_blocks(ambient_diffusion, blocks_x, blocks_y)
    shortwave_blocks = plane_blocks(solar_light, blocks_x, blocks_y)
    diffusion_each_tile = flat_mixer(
        thermal_tiles.astype(jnp.float32),
        spread_levels(ambient_diffusion_tiles.astype(jnp.float32), layer_tally),
    )
    payload = jnp.concatenate([thermal_tiles, diffusion_each_tile, shortwave_blocks], axis=1)
    holder_chip = tile_holder_rank.reshape(tile_summation)
    order = jnp.arange(tile_summation, dtype=jnp.int32)
    same = (holder_chip[:, None] == holder_chip[None, :]) & (order[None, :] < order[:, None])
    rank = jnp.sum(same.astype(jnp.int32), axis=1)
    position_summation = solute_amounts.shape[2]
    device_groups = lax.axis_size(GY)
    slot_limit = position_summation // device_groups
    target_owner = holder_chip * slot_limit + rank
    selection_mask = (
        lax.broadcasted_iota(jnp.int32, (position_summation, tile_summation), 0)
        == target_owner[None, :]
    )
    select_b = selection_mask.astype(jnp.bfloat16)
    packed = jnp.einsum("sb,bf->sf", select_b, payload, preferred_element_type=jnp.float32).astype(
        jnp.bfloat16
    )
    packed_count = jnp.sum(selection_mask.astype(jnp.int32) * depth_block[None, :], axis=1)
    arrived_tiles, received_count = (
        lax.all_to_all(
            packed.reshape(device_groups, slot_limit, packed.shape[1]),
            GY,
            split_axis=0,
            concat_axis=0,
            tiled=True,
        ),
        lax.all_to_all(
            packed_count.reshape(device_groups, slot_limit),
            GY,
            split_axis=0,
            concat_axis=0,
            tiled=True,
        ),
    )
    arrived_tiles = arrived_tiles.reshape(position_summation, arrived_tiles.shape[2])
    tile_amount = received_count.reshape(position_summation)
    thermal_at_position = arrived_tiles[:, :flat_width]
    diffusion_at_position = arrived_tiles[:, flat_width : 2 * flat_width]
    solar_at_position = arrived_tiles[:, 2 * flat_width :]
    surface = spread_levels(solar_at_position.astype(jnp.float32), layer_tally)
    amounts_on_chip = solute_amounts.reshape(
        position_summation, solute_amounts.shape[3], flat_width
    )
    valid, active = flat_validity(tile_amount, flat_width)
    old_local = totals(amounts_on_chip, valid)
    cells_local = jnp.sum(valid)
    new, heat = column_step(
        thermal_at_position,
        diffusion_at_position,
        surface,
        valid,
        active,
        amounts_on_chip,
        reaction_rates,
        layer_tally,
    )
    old_total, cells, new_total = (
        by_axis(old_local, GX_GY),
        by_axis(cells_local, GX_GY),
        by_axis(totals(new, valid), GX_GY),
    )
    shift = (old_total - new_total) / jnp.maximum(cells, 1.0)
    solute_final = jnp.where(
        valid[:, None] > 0, new + shift[None, :, None], amounts_on_chip
    ).reshape(solute_amounts.shape)
    returned_blocks = lax.all_to_all(
        heat.reshape(device_groups, slot_limit, flat_width),
        GY,
        split_axis=0,
        concat_axis=0,
        tiled=True,
    )
    returned_blocks = returned_blocks.reshape(position_summation, flat_width)
    heat_blocks = jnp.einsum(
        "sb,sf->bf", select_b, returned_blocks, preferred_element_type=jnp.float32
    )
    warming_each_site = (
        heat_blocks.reshape(blocks_x, blocks_y, layer_tally, 8, 8)
        .transpose(2, 0, 3, 1, 4)
        .reshape(layer_tally, span_east, span_north)
    )
    thermal_final = advanced_verticals + WARMING_SCALE * warming_each_site
    return (thermal_final, solute_final)


def solution(mesh):
    finer = Mesh(mesh.devices.reshape(4, 2, 4, 4), ("gx_0", "gx_1", "gy_0", "gy_1"))
    in_specs = (
        P(None, GX, GY),
        P(GX, GY),
        P(GX, GY),
        P(GX, GY, None),
        P(GX, GY, None),
        P(GX, GY, None, None),
        P(GX, GY, None, None, None),
        P(),
    )
    out_specs = (P(None, GX, GY), P(GX, GY, None, None, None))
    return jax.shard_map(
        on_device, mesh=finer, in_specs=in_specs, out_specs=out_specs, check_vma=False
    )
```

profile of v0, /device:TPU:0, one launch (start us, length us, event | category | flops | bytes accessed | tf_op | source)
XLA Modules:
  0.0 178.2 jit_solution(17803232174242923997)
XLA Ops:
  0.6 0.7 convert_reduce_fusion.1
  1.6 1.5 fusion.17
  3.5 3.5 %collective-permute-start = (f32[33,32,1]{0,1,2:T(8,128)S(1)}, f32[33,32,1]{0,1,2:T(8,128)S(1)}, u32[]{:S(2)}, u32[]{:S(2)}) collective-permute-start(f32[33,32,1]{0,1,2:T(8,128)S(1)} %copy.106), channel_id=1, source_target_pairs={{0,1},{1,2},{2,3},{3,4},{4,5},{5,6},{6,7},{7,8},{8,9},{9,10},{10,1... | collective-permute-start | bytes 12680 | tf_op jit(solution)/shard_map/ppermute | solution.py:26
  7.4 1.3 collective-permute-start.3
  8.7 1.0 fusion.37
  9.7 1.5 collective-permute-start.1
  11.2 1.3 collective-permute-start.2
  12.5 0.7 multiply_bitcast_fusion.1
  13.2 0.9 convert_reduce_fusion
  14.1 0.7 multiply_add_fusion
  14.8 0.7 all_to_all.12
  15.5 8.9 %all-to-all-start = ((s32[16,1,8]{2,1,0:T(1,128)}), s32[16,1,8]{2,1,0:T(1,128)S(1)}, u32[]{:S(2)}, u32[]{:S(2)}) async-start(s32[16,1,8]{2,1,0:T(1,128)} %bitcast.8), calls=%async_computation | async-start | bytes 16384 | tf_op jit(solution)/shard_map/all_to_all | solution.py:193
  24.4 4.8 %fusion.9 = f32[128,1,2048]{2,1,0:T(1,128)S(1)} fusion(f32[128,8,2048]{2,1,0:T(8,128)} %bitcast.77), kind=kLoop, calls=%fused_computation.21 | loop fusion | flops 524288 | bytes 2097152 | tf_op jit(solution)/shard_map/add | solution.py:101
  31.4 1.3 copy.107
  32.7 1.1 pad.13
  33.9 1.3 copy.109
  35.2 1.1 pad.14
  36.6 2.0 %fusion.45 = (bf16[32,32,128]{2,1,0:T(8,128)(2,1)}, f32[32,32,128]{2,1,0:T(8,128)}) fusion(f32[32,32,128]{2,1,0:T(8,128)S(1)} %copy-done.1, f32[33,34,1]{2,1,0:T(8,128)S(1)} %pad.14, f32[33,1,128]{2,1,0:T(1,128)S(1)} %collective-permute-done.2, f32[1,32,128]{2,1,0:T(8,128)S(1)} %copy.105, f32[33,1,128]{2,1,0:T(1,128)S(1)} %collective-permute-done.1, ...), kind=kLoop, calls=%fused_computation.108 | loop fusion | flops 3538944 | bytes 3991312 | tf_op jit(solution)/shard_map/convert_element_type | solution.py:155
  38.6 2.3 %copy.111 = bf16[32,32,128]{0,2,1:T(8,128)(2,1)} copy(bf16[32,32,128]{2,1,0:T(8,128)(2,1)} %get-tuple-element.20) | data formatting | bytes 524288 | tf_op jit(solution)/shard_map/convert_element_type | solution.py:155
  40.9 4.9 %copy.112 = bf16[4,16,32,8,8]{1,0,4,3,2:T(4,128)(2,1)S(1)} copy(bf16[4,16,32,8,8]{2,4,1,3,0:T(8,128)(2,1)} %bitcast.83) | data formatting | bytes 524288 | tf_op jit(solution)/shard_map/transpose | solution.py:158
  45.9 1.7 reshape.250
  47.7 1.2 slice.138
  48.9 0.7 slice.139
  49.6 1.3 fusion.14
  50.9 2.5 %convolution_convert_fusion = bf16[128,4160]{0,1:T(8,128)(2,1)} fusion(bf16[64,64]{0,1:T(8,128)(2,1)S(1)} %reshape.252, bf16[64,2048]{0,1:T(8,128)(2,1)S(1)} %fusion.14, bf16[64,2048]{0,1:T(8,128)(2,1)} %reshape.250, s32[64]{0:T(128)S(1)} %multiply_add_fusion), kind=kOutput, calls=%fused_computation.8 | convolution fusion | flops 70295552 | bytes 1597696 | tf_op jit(solution)/shard_map/sb,bf->sf/dot_general | solution.py:181
  53.5 2.4 %copy.115 = bf16[128,4160]{1,0:T(8,128)(2,1)} copy(bf16[128,4160]{0,1:T(8,128)(2,1)} %convolution_convert_fusion) | data formatting | bytes 2129920 | tf_op jit(solution)/shard_map/convert_element_type | solution.py:181
  55.8 7.3 %all-to-all-start.1 = ((bf16[16,8,4160]{2,1,0:T(8,128)(2,1)}), bf16[16,8,4160]{2,1,0:T(8,128)(2,1)}, u32[]{:S(2)}, u32[]{:S(2)}) async-start(bf16[16,8,4160]{2,1,0:T(8,128)(2,1)} %bitcast.82), calls=%async_computation.1 | async-start | bytes 2162688 | tf_op jit(solution)/shard_map/all_to_all | solution.py:186
  63.3 9.4 %slice.148 = f32[128,8,1984]{2,1,0:T(8,128)} slice(f32[128,8,2048]{2,1,0:T(8,128)} %bitcast.78), slice={[0:128], [0:8], [64:2048]} | slice | bytes 16252928 | tf_op jit(solution)/shard_map/slice | solution.py:58
  72.6 2.1 %slice.149 = f32[128,8,64]{2,1,0:T(8,128)} slice(f32[128,8,2048]{2,1,0:T(8,128)} %bitcast.79), slice={[0:128], [0:8], [1984:2048]} | slice | bytes 524288 | tf_op jit(solution)/shard_map/slice | solution.py:58
  74.7 0.9 slice.146
  76.1 0.6 reduce.7
  76.8 1.3 fusion.16
  78.1 2.9 %all-to-all-done.1 = bf16[16,8,4160]{2,1,0:T(8,128)(2,1)} async-done(((bf16[16,8,4160]{2,1,0:T(8,128)(2,1)}), bf16[16,8,4160]{2,1,0:T(8,128)(2,1)}, u32[]{:S(2)}, u32[]{:S(2)}) %all-to-all-start.1) | async-done | bytes 1064992 | tf_op jit(solution)/shard_map/all_to_all | solution.py:186
  81.0 0.8 slice.140
  82.0 1.4 copy.117
  83.3 4.9 %add_divide_fusion = (f32[128,2048]{1,0:T(8,128)S(1)}, bf16[16,8,2048]{2,1,0:T(8,128)(2,1)}, f32[128,2048]{1,0:T(8,128)}, f32[]{:T(128)}, f32[128,2048]{1,0:T(8,128)S(1)}) fusion(f32[128,2048]{1,0:T(8,128)} %copy.117, f32[128,2048]{1,0:T(8,128)} %copy-done.4, f32[128,1024]{1,0:T(8,128)} %slice.146, bf16[128,4160]{1,0:T(8,128)(2,1)} %bitcast.15, ...), kind=kLoop, calls=%fused_computation.29 | loop fusion | flops 5505023 | bytes 8405508 | tf_op jit(solution)/shard_map/div | solution.py:106
  88.3 4.6 %all-to-all-start.2 = ((bf16[16,8,2048]{2,1,0:T(8,128)(2,1)}), bf16[16,8,2048]{2,1,0:T(8,128)(2,1)S(1)}, u32[]{:S(2)}, u32[]{:S(2)}) async-start(bf16[16,8,2048]{2,1,0:T(8,128)(2,1)} %get-tuple-element.23), calls=%async_computation.2 | async-start | bytes 1048576 | tf_op jit(solution)/shard_map/all_to_all | solution.py:232
  92.9 8.0 %fusion = f32[128,8,2048]{2,1,0:T(8,128)S(1)} fusion(f32[128,8,64]{2,1,0:T(8,128)} %slice.149, f32[128,8,1984]{2,1,0:T(8,128)} %slice.148, f32[128,2048]{1,0:T(8,128)} %get-tuple-element.24, f32[1,1,128,8,2048]{4,3,2,1,0:T(8,128)} %param.14), kind=kLoop, calls=%fused_computation.1 | loop fusion | flops 6291456 | bytes 26214400 | tf_op jit(solution)/shard_map/mul | solution.py:110
  100.9 24.2 %multiply_reduce_fusion = (f32[8]{0:T(128)S(1)}, f32[8]{0:T(128)S(1)}, f32[128,8,2048]{2,1,0:T(8,128)}) fusion(f32[128,2048]{1,0:T(8,128)S(1)} %copy-done.5, f32[1,1,128,8,2048]{4,3,2,1,0:T(8,128)} %param.14, f32[8,8]{1,0:T(8,128)S(1)} %copy-done, f32[128,2048]{1,0:T(8,128)S(1)} %get-tuple-element.22, f32[128,8,2048]{2,1,0:T(8,128)S(1)} %fusion, ...), kind=kOutput, calls=%fused_computation.6 | convolution fusion | flops 220200944 | bytes 36438336 | tf_op jit(solution)/shard_map/rs,nsf->nrf/dot_general | solution.py:107
  125.1 13.9 %all-reduce.10 = (f32[8]{0:T(128)S(1)}, f32[8]{0:T(128)S(1)}, f32[]{:T(128)}) all-reduce(f32[8]{0:T(128)S(1)} %get-tuple-element.7, f32[8]{0:T(128)S(1)} %get-tuple-element.6, f32[]{:T(128)} %get-tuple-element.29), channel_id=1, replica_groups=mesh['gx_0'=4,'gx_1'=2,'gy_0'=4,'gy_1'=4] {'gx_0'}, use_global_device_ids=true, to_apply=%region_3.4 | all-reduce | flops 17 | bytes 136 | tf_op jit(solution)/shard_map/psum | solution.py:40
  139.0 3.1 %all-reduce.11 = (f32[8]{0:T(128)S(1)}, f32[8]{0:T(128)S(1)}, f32[]{:T(128)}) all-reduce(f32[8]{0:T(128)S(1)} %get-tuple-element.14, f32[8]{0:T(128)S(1)} %get-tuple-element.15, f32[]{:T(128)} %get-tuple-element.16), channel_id=1, replica_groups=mesh['gx_0'=4,'gx_1'=2,'gy_0'=4,'gy_1'=4] {'gx_1'}, use_global_device_ids=true, to_apply=%region_4.5 | all-reduce | flops 17 | bytes 136 | tf_op jit(solution)/shard_map/psum | solution.py:40
  142.1 11.5 %all-reduce.9 = (f32[8]{0:T(128)S(1)}, f32[8]{0:T(128)S(1)}, f32[]{:T(128)}) all-reduce(f32[8]{0:T(128)S(1)} %get-tuple-element.17, f32[8]{0:T(128)S(1)} %get-tuple-element.18, f32[]{:T(128)} %get-tuple-element.19), channel_id=1, replica_groups=mesh['gx_0'=4,'gx_1'=2,'gy_0'=4,'gy_1'=4] {'gy_0'}, use_global_device_ids=true, to_apply=%region_5.6 | all-reduce | flops 17 | bytes 136 | tf_op jit(solution)/shard_map/psum | solution.py:40
  153.6 11.0 %all-reduce.8 = (f32[8]{0:T(128)S(1)}, f32[8]{0:T(128)S(1)}, f32[]{:T(128)}) all-reduce(f32[8]{0:T(128)S(1)} %get-tuple-element.11, f32[8]{0:T(128)S(1)} %get-tuple-element.12, f32[]{:T(128)} %get-tuple-element.13), channel_id=1, replica_groups=mesh['gx_0'=4,'gx_1'=2,'gy_0'=4,'gy_1'=4] {'gy_1'}, use_global_device_ids=true, to_apply=%region_6.7 | all-reduce | flops 17 | bytes 136 | tf_op jit(solution)/shard_map/psum | solution.py:40
  165.2 9.3 %select_bitcast_fusion = f32[1,1,128,8,2048]{4,3,2,1,0:T(8,128)} fusion(f32[128,8,2048]{2,1,0:T(8,128)} %get-tuple-element.33, f32[8]{0:T(128)S(1)} %subtract_divide_fusion, pred[128,2048]{1,0:T(8,128)(4,1)S(1)} %get-tuple-element.31, f32[1,1,128,8,2048]{4,3,2,1,0:T(8,128)} %param.14), kind=kLoop, calls=%fused_computation.5 | loop fusion | flops 4194304 | bytes 25428000 | tf_op jit(solution)/shard_map/reshape | solution.py:231
  174.7 1.0 multiply_bitcast_fusion
  175.7 0.9 copy.121
  176.6 0.7 copy.122
  177.3 0.9 add.145
  (58 shorter events, 4.8 us)
Async XLA Ops:
  0.6 100.2 %copy-start = (f32[8,8]{1,0:T(8,128)S(1)}, f32[8,8]{1,0:T(8,128)}, u32[]{:S(2)}) copy-start(f32[8,8]{1,0:T(8,128)} %param.15) | copy-start | bytes 772
  3.5 27.9 %collective-permute-start = (f32[33,32,1]{0,1,2:T(8,128)S(1)}, f32[33,32,1]{0,1,2:T(8,128)S(1)}, u32[]{:S(2)}, u32[]{:S(2)}) collective-permute-start(f32[33,32,1]{0,1,2:T(8,128)S(1)} %copy.106), channel_id=1, source_target_pairs={{0,1},{1,2},{2,3},{3,4},{4,5},{5,6},{6,7},{7,8},{8,9},{9,10},{10,1... | collective-permute-start | bytes 12680 | tf_op jit(solution)/shard_map/ppermute | solution.py:26
  7.4 26.4 %collective-permute-start.3 = (f32[33,32,1]{0,1,2:T(8,128)S(1)}, f32[33,32,1]{0,1,2:T(8,128)S(1)}, u32[]{:S(2)}, u32[]{:S(2)}) collective-permute-start(f32[33,32,1]{0,1,2:T(8,128)S(1)} %copy.108), channel_id=1, source_target_pairs={{1,0},{2,1},{3,2},{4,3},{5,4},{6,5},{7,6},{8,7},{9,8},{10,9},{11,1... | collective-permute-start | bytes 12680 | tf_op jit(solution)/shard_map/ppermute | solution.py:27
  9.7 26.6 %collective-permute-start.1 = (f32[33,1,128]{2,1,0:T(1,128)S(1)}, f32[33,1,128]{2,1,0:T(1,128)S(1)}, u32[]{:S(2)}, u32[]{:S(2)}) collective-permute-start(f32[33,1,128]{2,1,0:T(1,128)S(1)} %get-tuple-element.27), channel_id=1, source_target_pairs={{0,16},{16,32},{32,48},{48,64},{64,80},{80,96},{96,112},{1,17},{17... | collective-permute-start | bytes 50696 | tf_op jit(solution)/shard_map/ppermute | solution.py:26
  11.2 25.2 %collective-permute-start.2 = (f32[33,1,128]{2,1,0:T(1,128)S(1)}, f32[33,1,128]{2,1,0:T(1,128)S(1)}, u32[]{:S(2)}, u32[]{:S(2)}) collective-permute-start(f32[33,1,128]{2,1,0:T(1,128)S(1)} %get-tuple-element.28), channel_id=1, source_target_pairs={{16,0},{32,16},{48,32},{64,48},{80,64},{96,80},{112,96},{17,1},{33... | collective-permute-start | bytes 50696 | tf_op jit(solution)/shard_map/ppermute | solution.py:27
  15.5 40.3 %all-to-all-start = ((s32[16,1,8]{2,1,0:T(1,128)}), s32[16,1,8]{2,1,0:T(1,128)S(1)}, u32[]{:S(2)}, u32[]{:S(2)}) async-start(s32[16,1,8]{2,1,0:T(1,128)} %bitcast.8), calls=%async_computation | async-start | bytes 16384 | tf_op jit(solution)/shard_map/all_to_all | solution.py:193
  24.4 6.1 %copy-start.7 = (bf16[32,128]{1,0:T(8,128)(2,1)S(1)}, bf16[32,128]{1,0:T(8,128)(2,1)}, u32[]{:S(2)}) copy-start(bf16[32,128]{1,0:T(8,128)(2,1)} %param.9) | copy-start | bytes 24580
  29.2 1.7 copy-start.8
  30.1 6.3 %copy-start.1 = (f32[32,32,128]{2,1,0:T(8,128)S(1)}, f32[32,32,128]{2,1,0:T(8,128)}, u32[]{:S(2)}) copy-start(f32[32,32,128]{2,1,0:T(8,128)} %param.8) | copy-start | bytes 1572868
  30.5 10.5 %copy-start.2 = (f32[128,2048]{1,0:T(8,128)}, f32[128,2048]{1,0:T(8,128)S(1)}, u32[]{:S(2)}) copy-start(f32[128,2048]{1,0:T(8,128)S(1)} %pad_add_fusion.2) | copy-start | bytes 3145732
  47.7 15.5 %copy-start.3 = (f32[128,2048]{1,0:T(8,128)S(1)}, f32[128,2048]{1,0:T(8,128)}, u32[]{:S(2)}) copy-start(f32[128,2048]{1,0:T(8,128)} %copy-done.2) | copy-start | bytes 3145732
  47.7 15.5 %slice-start = ((f32[128,2048]{1,0:T(8,128)}), f32[128,1536]{1,0:T(8,128)S(1)}, s32[]{:S(2)}) async-start(f32[128,2048]{1,0:T(8,128)} %copy-done.2), calls=%async_computation.3 | async-start | bytes 1572864 | tf_op jit(solution)/shard_map/slice | solution.py:70
  55.8 25.1 %all-to-all-start.1 = ((bf16[16,8,4160]{2,1,0:T(8,128)(2,1)}), bf16[16,8,4160]{2,1,0:T(8,128)(2,1)}, u32[]{:S(2)}, u32[]{:S(2)}) async-start(bf16[16,8,4160]{2,1,0:T(8,128)(2,1)} %bitcast.82), calls=%async_computation.1 | async-start | bytes 2162688 | tf_op jit(solution)/shard_map/all_to_all | solution.py:186
  63.2 11.5 %copy-start.4 = (f32[128,2048]{1,0:T(8,128)}, f32[128,2048]{1,0:T(8,128)S(1)}, u32[]{:S(2)}) copy-start(f32[128,2048]{1,0:T(8,128)S(1)} %pad_add_fusion.1) | copy-start | bytes 3145732
  88.3 86.2 %all-to-all-start.2 = ((bf16[16,8,2048]{2,1,0:T(8,128)(2,1)}), bf16[16,8,2048]{2,1,0:T(8,128)(2,1)S(1)}, u32[]{:S(2)}, u32[]{:S(2)}) async-start(bf16[16,8,2048]{2,1,0:T(8,128)(2,1)} %get-tuple-element.23), calls=%async_computation.2 | async-start | bytes 1048576 | tf_op jit(solution)/shard_map/all_to_all | solution.py:232
  92.9 8.0 %copy-start.5 = (f32[128,2048]{1,0:T(8,128)S(1)}, f32[128,2048]{1,0:T(8,128)}, u32[]{:S(2)}) copy-start(f32[128,2048]{1,0:T(8,128)} %get-tuple-element.32) | copy-start | bytes 3145732
  174.4 2.9 %copy-start.6 = (f32[32,32,128]{2,1,0:T(8,128)S(1)}, f32[32,32,128]{2,1,0:T(8,128)}, u32[]{:S(2)}) copy-start(f32[32,32,128]{2,1,0:T(8,128)} %get-tuple-element.21) | copy-start | bytes 1572868
where the time goes:
time: 179 us; the launch traced here: 178 us
  other arithmetic  39.7 us (22%)
  blocking collectives  39.5 us (22%)
  local copies, waits for them, and re-layouts  38.5 us (22%)
  starting transfers between devices  28.2 us (16%)
  matrix products  27.8 us (16%)
  waiting for transfers between devices  2.92 us (2%)
    psum x4, blocking collectives, by_axis(): shard = lax.psum(shard, axis)  39.5 us
    dot_general x1, matrix products, column_step(): jnp.einsum('rs,nsf->nrf', reaction_rates, amounts_on_chip, precision=lax....  24.2 us
    slice x4, local copies, waits for them, and re-layouts, level_below(): return jnp.concatenate([values[..., 64:], values[..., -64:]], axis=-1)  13.4 us
    reshape x1, other arithmetic, on_device(): solute_final = jnp.where(valid[:, None] > 0, new + shift[None, :, None],...  9.28 us
    all_to_all x1, starting transfers between devices, on_device(): lax.all_to_all(packed_count.reshape(device_groups, slot_limit), GY, split...  8.86 us
    mul x1, other arithmetic, column_step(): (kappa_flat.astype(jnp.float32) * active)[:, None]  7.96 us
    all_to_all x1, starting transfers between devices, on_device(): lax.all_to_all(packed.reshape(device_groups, slot_limit, packed.shape[1])...  7.27 us
    transpose x1, local copies, waits for them, and re-layouts, on_device(): thermal_tiles = dispatched.reshape(layer_tally, blocks_x, 8, blocks_y, 8)...  4.95 us
  transfers between devices with their start and end apart: 7, of which 1 were waited for; matrix products, arithmetic and copies ran while one was open for 51% of the time, Pallas kernels for 0%

commit v1 on v0

--- a/solution.py
+++ b/solution.py
@@ -37,7 +37,7 @@
 
 def by_axis(shard, axes):
     for axis in axes:
-        shard = lax.psum(shard, axis)
+        shard = jnp.sum(lax.all_gather(shard, axis), axis=0)
     return shard
 
 

time: 179 us -> 185 us (1.034)
  local copies, waits for them, and re-layouts: 38.5 us -> 49 us
  waiting for transfers between devices: 2.92 us -> 0.02 us
  between operations: 1.63 us -> 4.44 us
  matrix products: 27.8 us -> 25.2 us
  blocking collectives: 39.5 us -> 37.5 us
    psum x4 -> x0, blocking collectives: 39.5 us -> none  [by_axis(): shard = lax.psum(shard, axis)]
    unnamed x0 -> x4, blocking collectives: none -> 37.5 us
    unnamed x20 -> x60, local copies, waits for them, and re-layouts: 0.47 us -> 10.4 us
    all_to_all x1, waiting for transfers between devices: 2.91 us -> 0.01 us  [on_device(): lax.all_to_all(packed.reshape(device_groups, slot_limit, packed.shape[1])...]
    reduce_sum x0 -> x12, other arithmetic: none -> 2.78 us  [by_axis(): shard = jnp.sum(lax.all_gather(shard, axis), axis=0)]
    dot_general x1, matrix products: 24.2 us -> 21.6 us  [column_step(): jnp.einsum('rs,nsf->nrf', reaction_rates, amounts_on_chip, precision=lax....]
  transfers between devices with their start and end apart: 7 -> 7, of which waited for: 1 -> 0; matrix products, arithmetic and copies ran while one was open for 51% -> 33% of each run, Pallas kernels for 0% -> 0%
where the time goes in v1:
time: 185 us; the launch traced here: 184 us
  local copies, waits for them, and re-layouts  49 us (26%)
  other arithmetic  40.5 us (22%)
  blocking collectives  37.5 us (20%)
  starting transfers between devices  27.2 us (15%)
  matrix products  25.2 us (14%)
  between operations  4.44 us (2%)
    unnamed x4, blocking collectives  37.5 us
    dot_general x1, matrix products, column_step(): jnp.einsum('rs,nsf->nrf', reaction_rates, amounts_on_chip, precision=lax....  21.6 us
    slice x4, local copies, waits for them, and re-layouts, level_below(): return jnp.concatenate([values[..., 64:], values[..., -64:]], axis=-1)  13.4 us
    unnamed x60, local copies, waits for them, and re-layouts  10.4 us
    reshape x1, other arithmetic, on_device(): solute_final = jnp.where(valid[:, None] > 0, new + shift[None, :, None],...  9.28 us
    all_to_all x1, starting transfers between devices, on_device(): lax.all_to_all(packed_count.reshape(device_groups, slot_limit), GY, split...  8.86 us
    all_to_all x1, starting transfers between devices, on_device(): lax.all_to_all(packed.reshape(device_groups, slot_limit, packed.shape[1])...  7.27 us
    mul x1, other arithmetic, column_step(): (kappa_flat.astype(jnp.float32) * active)[:, None]  7.26 us
  transfers between devices with their start and end apart: 7, of which 0 were waited for; matrix products, arithmetic and copies ran while one was open for 33% of the time, Pallas kernels for 0%

profile of v1, /device:TPU:0, one launch (start us, length us, event | category | flops | bytes accessed | tf_op | source)
XLA Modules:
  0.0 183.9 jit_solution(6688187778934899916)
XLA Ops:
  0.6 0.7 convert_reduce_fusion.1
  1.6 1.5 fusion.17
  3.5 3.5 %collective-permute-start = (f32[33,32,1]{0,1,2:T(8,128)S(1)}, f32[33,32,1]{0,1,2:T(8,128)S(1)}, u32[]{:S(2)}, u32[]{:S(2)}) collective-permute-start(f32[33,32,1]{0,1,2:T(8,128)S(1)} %copy.106), channel_id=1, source_target_pairs={{0,1},{1,2},{2,3},{3,4},{4,5},{5,6},{6,7},{7,8},{8,9},{9,10},{10,1... | collective-permute-start | bytes 12680 | tf_op jit(solution)/shard_map/ppermute | solution.py:26
  7.4 1.3 collective-permute-start.3
  8.7 1.0 fusion.37
  9.7 1.5 collective-permute-start.1
  11.2 1.3 collective-permute-start.2
  13.2 0.9 convert_reduce_fusion
  14.8 0.7 all_to_all.12
  15.5 8.9 %all-to-all-start = ((s32[16,1,8]{2,1,0:T(1,128)}), s32[16,1,8]{2,1,0:T(1,128)S(1)}, u32[]{:S(2)}, u32[]{:S(2)}) async-start(s32[16,1,8]{2,1,0:T(1,128)} %bitcast.8), calls=%async_computation | async-start | bytes 16384 | tf_op jit(solution)/shard_map/all_to_all | solution.py:193
  24.4 4.8 %fusion.9 = f32[128,1,2048]{2,1,0:T(1,128)S(1)} fusion(f32[128,8,2048]{2,1,0:T(8,128)} %bitcast.89), kind=kLoop, calls=%fused_computation.21 | loop fusion | flops 524288 | bytes 2097152 | tf_op jit(solution)/shard_map/add | solution.py:101
  31.4 1.3 copy.107
  32.7 1.1 pad.13
  33.9 1.3 copy.109
  35.2 1.1 pad.14
  36.6 2.0 %fusion.45 = (bf16[32,32,128]{2,1,0:T(8,128)(2,1)}, f32[32,32,128]{2,1,0:T(8,128)}) fusion(f32[32,32,128]{2,1,0:T(8,128)S(1)} %copy-done.2, f32[33,34,1]{2,1,0:T(8,128)S(1)} %pad.14, f32[33,1,128]{2,1,0:T(1,128)S(1)} %collective-permute-done.2, f32[1,32,128]{2,1,0:T(8,128)S(1)} %copy.105, f32[33,1,128]{2,1,0:T(1,128)S(1)} %collective-permute-done.1, ...), kind=kLoop, calls=%fused_computation.108 | loop fusion | flops 3538944 | bytes 3991312 | tf_op jit(solution)/shard_map/convert_element_type | solution.py:155
  38.6 2.3 %copy.111 = bf16[32,32,128]{0,2,1:T(8,128)(2,1)} copy(bf16[32,32,128]{2,1,0:T(8,128)(2,1)} %get-tuple-element.20) | data formatting | bytes 524288 | tf_op jit(solution)/shard_map/convert_element_type | solution.py:155
  40.9 4.9 %copy.112 = bf16[4,16,32,8,8]{1,0,4,3,2:T(4,128)(2,1)S(1)} copy(bf16[4,16,32,8,8]{2,4,1,3,0:T(8,128)(2,1)} %bitcast.97) | data formatting | bytes 524288 | tf_op jit(solution)/shard_map/transpose | solution.py:158
  45.9 1.7 reshape.255
  47.7 1.2 slice.138
  48.9 0.7 slice.139
  49.6 1.3 fusion.14
  50.9 2.5 %convolution_convert_fusion = bf16[128,4160]{0,1:T(8,128)(2,1)} fusion(bf16[64,64]{0,1:T(8,128)(2,1)S(1)} %reshape.257, bf16[64,2048]{0,1:T(8,128)(2,1)S(1)} %fusion.14, bf16[64,2048]{0,1:T(8,128)(2,1)} %reshape.255, s32[64]{0:T(128)S(1)} %multiply_add_fusion), kind=kOutput, calls=%fused_computation.8 | convolution fusion | flops 70295552 | bytes 1597696 | tf_op jit(solution)/shard_map/sb,bf->sf/dot_general | solution.py:181
  53.5 2.4 %copy.115 = bf16[128,4160]{1,0:T(8,128)(2,1)} copy(bf16[128,4160]{0,1:T(8,128)(2,1)} %convolution_convert_fusion) | data formatting | bytes 2129920 | tf_op jit(solution)/shard_map/convert_element_type | solution.py:181
  55.8 7.3 %all-to-all-start.1 = ((bf16[16,8,4160]{2,1,0:T(8,128)(2,1)}), bf16[16,8,4160]{2,1,0:T(8,128)(2,1)}, u32[]{:S(2)}, u32[]{:S(2)}) async-start(bf16[16,8,4160]{2,1,0:T(8,128)(2,1)} %bitcast.96), calls=%async_computation.1 | async-start | bytes 2162688 | tf_op jit(solution)/shard_map/all_to_all | solution.py:186
  63.3 9.4 %slice.148 = f32[128,8,1984]{2,1,0:T(8,128)} slice(f32[128,8,2048]{2,1,0:T(8,128)} %bitcast.90), slice={[0:128], [0:8], [64:2048]} | slice | bytes 16252928 | tf_op jit(solution)/shard_map/slice | solution.py:58
  72.7 2.0 %slice.149 = f32[128,8,64]{2,1,0:T(8,128)} slice(f32[128,8,2048]{2,1,0:T(8,128)} %bitcast.91), slice={[0:128], [0:8], [1984:2048]} | slice | bytes 524288 | tf_op jit(solution)/shard_map/slice | solution.py:58
  74.7 0.8 slice.146
  82.3 0.8 slice.140
  83.3 1.4 copy.117
  84.6 4.6 %add_divide_fusion = (f32[128,2048]{1,0:T(8,128)S(1)}, bf16[16,8,2048]{2,1,0:T(8,128)(2,1)}, f32[128,2048]{1,0:T(8,128)S(1)}, f32[]{:T(128)}, f32[128,2048]{1,0:T(8,128)S(1)}) fusion(f32[128,2048]{1,0:T(8,128)} %copy.117, f32[128,2048]{1,0:T(8,128)} %copy-done.5, f32[128,1024]{1,0:T(8,128)} %slice.146, bf16[128,4160]{1,0:T(8,128)(2,1)} %bitcast.15, ...), kind=kLoop, calls=%fused_computation.29 | loop fusion | flops 5505023 | bytes 8405508 | tf_op jit(solution)/shard_map/div | solution.py:106
  89.3 7.3 %fusion = f32[128,8,2048]{2,1,0:T(8,128)} fusion(f32[128,8,64]{2,1,0:T(8,128)} %slice.149, f32[128,8,1984]{2,1,0:T(8,128)S(1)} %copy-done.1, f32[128,2048]{1,0:T(8,128)S(1)} %get-tuple-element.24, f32[1,1,128,8,2048]{4,3,2,1,0:T(8,128)} %param.14), kind=kLoop, calls=%fused_computation.1 | loop fusion | flops 6291456 | bytes 26214400 | tf_op jit(solution)/shard_map/mul | solution.py:110
  96.6 21.6 %multiply_reduce_fusion = (f32[8]{0:T(128)S(1)}, f32[8]{0:T(128)S(1)}, f32[128,8,2048]{2,1,0:T(8,128)}) fusion(f32[128,2048]{1,0:T(8,128)S(1)} %get-tuple-element.32, f32[1,1,128,8,2048]{4,3,2,1,0:T(8,128)S(1)} %bitcast.93, f32[8,8]{1,0:T(8,128)S(1)} %copy-done, f32[128,2048]{1,0:T(8,128)S(1)} %get-tuple-element.22, f32[128,8,2048]{2,1,0:T(8,128)} %fusion, ...), kind=kOutput, calls=%fused_computation.6 | convolution fusion | flops 220200944 | bytes 36438336 | tf_op jit(solution)/shard_map/rs,nsf->nrf/dot_general | solution.py:107
  118.7 1.4 dynamic-update-slice.8
  120.1 13.7 %all-reduce.22 = (f32[32]{0:T(128)S(1)}, f32[32]{0:T(128)S(1)}, f32[4]{0:T(128)S(1)}) all-reduce(f32[32]{0:T(128)S(1)} %dynamic-update-slice, f32[32]{0:T(128)S(1)} %dynamic-update-slice.4, f32[4]{0:T(128)S(1)} %dynamic-update-slice.8), channel_id=2, replica_groups=mesh['gx_0'=4,'gx_1'=2,'gy_0'=4,'gy_1'=4] {'gx_0'}, use_global_device_ids=true, to_apply=%add.8 | all-reduce | flops 68 | bytes 544
  135.1 1.4 dynamic-update-slice.9
  136.5 2.7 %all-reduce.23 = (f32[16]{0:T(128)S(1)}, f32[16]{0:T(128)S(1)}, f32[2]{0:T(128)S(1)}) all-reduce(f32[16]{0:T(128)S(1)} %dynamic-update-slice.1, f32[16]{0:T(128)S(1)} %dynamic-update-slice.5, f32[2]{0:T(128)S(1)} %dynamic-update-slice.9), channel_id=3, replica_groups=mesh['gx_0'=4,'gx_1'=2,'gy_0'=4,'gy_1'=4] {'gx_1'}, use_global_device_ids=true, to_apply=%add.9 | all-reduce | flops 34 | bytes 272
  140.5 1.4 dynamic-update-slice.10
  141.8 10.8 %all-reduce.21 = (f32[32]{0:T(128)S(1)}, f32[32]{0:T(128)S(1)}, f32[4]{0:T(128)S(1)}) all-reduce(f32[32]{0:T(128)S(1)} %dynamic-update-slice.2, f32[32]{0:T(128)S(1)} %dynamic-update-slice.6, f32[4]{0:T(128)S(1)} %dynamic-update-slice.10), channel_id=4, replica_groups=mesh['gx_0'=4,'gx_1'=2,'gy_0'=4,'gy_1'=4] {'gy_0'}, use_global_device_ids=true, to_apply=%add.10 | all-reduce | flops 68 | bytes 544
  153.9 1.4 dynamic-update-slice.11
  155.3 10.4 %all-reduce.20 = (f32[32]{0:T(128)S(1)}, f32[32]{0:T(128)S(1)}, f32[4]{0:T(128)S(1)}) all-reduce(f32[32]{0:T(128)S(1)} %dynamic-update-slice.3, f32[32]{0:T(128)S(1)} %dynamic-update-slice.7, f32[4]{0:T(128)S(1)} %dynamic-update-slice.11), channel_id=5, replica_groups=mesh['gx_0'=4,'gx_1'=2,'gy_0'=4,'gy_1'=4] {'gy_1'}, use_global_device_ids=true, to_apply=%add.11 | all-reduce | flops 68 | bytes 544
  165.8 3.6 %all-to-all-start.2 = ((bf16[16,8,2048]{2,1,0:T(8,128)(2,1)}), bf16[16,8,2048]{2,1,0:T(8,128)(2,1)S(1)}, u32[]{:S(2)}, u32[]{:S(2)}) async-start(bf16[16,8,2048]{2,1,0:T(8,128)(2,1)} %get-tuple-element.23), calls=%async_computation.2 | async-start | bytes 1048576 | tf_op jit(solution)/shard_map/all_to_all | solution.py:232
  169.4 0.7 reduce_sum.169
  170.8 9.3 %select_bitcast_fusion = f32[1,1,128,8,2048]{4,3,2,1,0:T(8,128)} fusion(f32[128,8,2048]{2,1,0:T(8,128)} %get-tuple-element.33, f32[8]{0:T(128)S(1)} %subtract_divide_fusion, pred[128,2048]{1,0:T(8,128)(4,1)S(1)} %get-tuple-element.31, f32[1,1,128,8,2048]{4,3,2,1,0:T(8,128)} %param.14), kind=kLoop, calls=%fused_computation.5 | loop fusion | flops 4194304 | bytes 25428000 | tf_op jit(solution)/shard_map/reshape | solution.py:231
  180.4 1.0 multiply_bitcast_fusion
  181.4 0.9 copy.121
  182.3 0.7 copy.122
  183.0 0.9 add.121
  (119 shorter events, 14.2 us)
Async XLA Ops:
  0.6 96.0 %copy-start = (f32[8,8]{1,0:T(8,128)S(1)}, f32[8,8]{1,0:T(8,128)}, u32[]{:S(2)}) copy-start(f32[8,8]{1,0:T(8,128)} %param.15) | copy-start | bytes 772
  3.5 27.9 %collective-permute-start = (f32[33,32,1]{0,1,2:T(8,128)S(1)}, f32[33,32,1]{0,1,2:T(8,128)S(1)}, u32[]{:S(2)}, u32[]{:S(2)}) collective-permute-start(f32[33,32,1]{0,1,2:T(8,128)S(1)} %copy.106), channel_id=1, source_target_pairs={{0,1},{1,2},{2,3},{3,4},{4,5},{5,6},{6,7},{7,8},{8,9},{9,10},{10,1... | collective-permute-start | bytes 12680 | tf_op jit(solution)/shard_map/ppermute | solution.py:26
  7.4 26.4 %collective-permute-start.3 = (f32[33,32,1]{0,1,2:T(8,128)S(1)}, f32[33,32,1]{0,1,2:T(8,128)S(1)}, u32[]{:S(2)}, u32[]{:S(2)}) collective-permute-start(f32[33,32,1]{0,1,2:T(8,128)S(1)} %copy.108), channel_id=1, source_target_pairs={{1,0},{2,1},{3,2},{4,3},{5,4},{6,5},{7,6},{8,7},{9,8},{10,9},{11,1... | collective-permute-start | bytes 12680 | tf_op jit(solution)/shard_map/ppermute | solution.py:27
  9.7 26.6 %collective-permute-start.1 = (f32[33,1,128]{2,1,0:T(1,128)S(1)}, f32[33,1,128]{2,1,0:T(1,128)S(1)}, u32[]{:S(2)}, u32[]{:S(2)}) collective-permute-start(f32[33,1,128]{2,1,0:T(1,128)S(1)} %get-tuple-element.27), channel_id=1, source_target_pairs={{0,16},{16,32},{32,48},{48,64},{64,80},{80,96},{96,112},{1,17},{17... | collective-permute-start | bytes 50696 | tf_op jit(solution)/shard_map/ppermute | solution.py:26
  11.2 25.2 %collective-permute-start.2 = (f32[33,1,128]{2,1,0:T(1,128)S(1)}, f32[33,1,128]{2,1,0:T(1,128)S(1)}, u32[]{:S(2)}, u32[]{:S(2)}) collective-permute-start(f32[33,1,128]{2,1,0:T(1,128)S(1)} %get-tuple-element.28), channel_id=1, source_target_pairs={{16,0},{32,16},{48,32},{64,48},{80,64},{96,80},{112,96},{17,1},{33... | collective-permute-start | bytes 50696 | tf_op jit(solution)/shard_map/ppermute | solution.py:27
  15.5 40.3 %all-to-all-start = ((s32[16,1,8]{2,1,0:T(1,128)}), s32[16,1,8]{2,1,0:T(1,128)S(1)}, u32[]{:S(2)}, u32[]{:S(2)}) async-start(s32[16,1,8]{2,1,0:T(1,128)} %bitcast.8), calls=%async_computation | async-start | bytes 16384 | tf_op jit(solution)/shard_map/all_to_all | solution.py:193
  24.4 6.1 %copy-start.7 = (bf16[32,128]{1,0:T(8,128)(2,1)S(1)}, bf16[32,128]{1,0:T(8,128)(2,1)}, u32[]{:S(2)}) copy-start(bf16[32,128]{1,0:T(8,128)(2,1)} %param.9) | copy-start | bytes 24580
  29.2 1.7 copy-start.8
  30.1 6.3 %copy-start.2 = (f32[32,32,128]{2,1,0:T(8,128)S(1)}, f32[32,32,128]{2,1,0:T(8,128)}, u32[]{:S(2)}) copy-start(f32[32,32,128]{2,1,0:T(8,128)} %param.8) | copy-start | bytes 1572868
  30.5 10.5 %copy-start.3 = (f32[128,2048]{1,0:T(8,128)}, f32[128,2048]{1,0:T(8,128)S(1)}, u32[]{:S(2)}) copy-start(f32[128,2048]{1,0:T(8,128)S(1)} %pad_add_fusion.2) | copy-start | bytes 3145732
  47.7 15.5 %copy-start.4 = (f32[128,2048]{1,0:T(8,128)S(1)}, f32[128,2048]{1,0:T(8,128)}, u32[]{:S(2)}) copy-start(f32[128,2048]{1,0:T(8,128)} %copy-done.3) | copy-start | bytes 3145732
  47.7 15.5 %slice-start.2 = ((f32[128,2048]{1,0:T(8,128)}), f32[128,1536]{1,0:T(8,128)S(1)}, s32[]{:S(2)}) async-start(f32[128,2048]{1,0:T(8,128)} %copy-done.3), calls=%async_computation.5 | async-start | bytes 1572864 | tf_op jit(solution)/shard_map/slice | solution.py:70
  55.8 26.5 %all-to-all-start.1 = ((bf16[16,8,4160]{2,1,0:T(8,128)(2,1)}), bf16[16,8,4160]{2,1,0:T(8,128)(2,1)}, u32[]{:S(2)}, u32[]{:S(2)}) async-start(bf16[16,8,4160]{2,1,0:T(8,128)(2,1)} %bitcast.96), calls=%async_computation.1 | async-start | bytes 2162688 | tf_op jit(solution)/shard_map/all_to_all | solution.py:186
  63.2 11.5 %copy-start.5 = (f32[128,2048]{1,0:T(8,128)}, f32[128,2048]{1,0:T(8,128)S(1)}, u32[]{:S(2)}) copy-start(f32[128,2048]{1,0:T(8,128)S(1)} %pad_add_fusion.1) | copy-start | bytes 3145732
  63.3 12.3 %copy-start.12 = (u32[128]{0:T(128)S(1)}, u32[128]{0:T(128)}, u32[]{:S(2)}) copy-start(u32[128]{0:T(128)} %constant.76) | copy-start | bytes 1540
  63.3 13.0 %copy-start.11 = (u32[128]{0:T(128)S(1)}, u32[128]{0:T(128)}, u32[]{:S(2)}) copy-start(u32[128]{0:T(128)} %constant.81) | copy-start | bytes 1540
  63.3 14.9 %copy-start.10 = (u32[128]{0:T(128)S(1)}, u32[128]{0:T(128)}, u32[]{:S(2)}) copy-start(u32[128]{0:T(128)} %constant.86) | copy-start | bytes 1540
  63.3 16.2 %copy-start.9 = (u32[128]{0:T(128)S(1)}, u32[128]{0:T(128)}, u32[]{:S(2)}) copy-start(u32[128]{0:T(128)} %constant.91) | copy-start | bytes 1540
  84.6 4.7 %copy-start.1 = (f32[128,8,1984]{2,1,0:T(8,128)S(1)}, f32[128,8,1984]{2,1,0:T(8,128)}, u32[]{:S(2)}) copy-start(f32[128,8,1984]{2,1,0:T(8,128)} %slice.148) | copy-start | bytes 24379396
  84.6 11.9 %slice-start = ((s8[8388608]{0:T(1024)(128)(4,1)}), s8[4194304]{0:T(1024)(128)(4,1)S(1)}, s32[]{:S(2)}) async-start(s8[8388608]{0:T(1024)(128)(4,1)} %bitcast.92), calls=%async_computation.3 | async-start | bytes 8388608
  89.3 7.3 %slice-start.1 = ((s8[8388608]{0:T(1024)(128)(4,1)}), s8[4194304]{0:T(1024)(128)(4,1)S(1)}, s32[]{:S(2)}) async-start(s8[8388608]{0:T(1024)(128)(4,1)} %bitcast.92), calls=%async_computation.4 | async-start | bytes 8388608
  165.8 14.3 %all-to-all-start.2 = ((bf16[16,8,2048]{2,1,0:T(8,128)(2,1)}), bf16[16,8,2048]{2,1,0:T(8,128)(2,1)S(1)}, u32[]{:S(2)}, u32[]{:S(2)}) async-start(bf16[16,8,2048]{2,1,0:T(8,128)(2,1)} %get-tuple-element.23), calls=%async_computation.2 | async-start | bytes 1048576 | tf_op jit(solution)/shard_map/all_to_all | solution.py:232
  180.1 2.9 %copy-start.6 = (f32[32,32,128]{2,1,0:T(8,128)S(1)}, f32[32,32,128]{2,1,0:T(8,128)}, u32[]{:S(2)}) copy-start(f32[32,32,128]{2,1,0:T(8,128)} %get-tuple-element.21) | copy-start | bytes 1572868
